TPU v7x, 256 devices: a whole 4x4x8 slice. The times are simulated.
256 devices in a mesh: seq: 64 (over z, x, core), head: 4 (over y).
Axes of the slice: x: 4, y: 4, z: 8, core: 2. Of those that a mesh axis runs over, the one named last changes fastest.
Arguments:
- qk: bfloat16 [65536, 2048], P('seq', 'head'), may hold values from -8 to 8
- values: bfloat16 [65536, 2048], P('seq', 'head'), may hold values from -6 to 6
- out_weight: bfloat16 [2048, 2048], P('head'), may hold values from -0.125 to 0.125
- out_cotangent: bfloat16 [65536, 2048], P('seq', 'head'), may hold values from -6 to 6
- cluster_ids: int32 [512, 16], P(None, 'head'), may hold values from 0 to 127, as said below
Outputs:
- output: bfloat16 [65536, 2048], P('seq', 'head')
- grad_qk: bfloat16 [65536, 2048], P('seq', 'head')
- grad_values: bfloat16 [65536, 2048], P('seq', 'head')
Inputs may be any that keep to these rules, and one draw needn't show every extreme that they name: `cluster_ids`: call c // 2 the owner of cluster c. Over the blocks of one seq index and the heads of one head index, at most 2 name clusters of one owner, and exactly 2 for some owner. For every head, the clusters of each owner hold exactly 8 blocks together, and some cluster holds all 8.
All inputs are finite; a program needn't handle non-finite values.
Results may differ from a plain program's by a relative error of at most 0.013.
Values may be sent and summed in bfloat16 or wider, within the bound.
A program may use at most 128 MiB of HBM per device.

v0:
```python
import jax
import jax.numpy as jnp
from jax import lax
from jax.sharding import PartitionSpec as P

BLOCK = 128
CL_OWN = 2
NEG_FILL = -1e30


def unit_forward(tokens_x, tokens_v, group):
    row_count = tokens_x.shape[0]
    block_rows = row_count // group.shape[0]
    inv_root = tokens_x.shape[1] ** (-0.5)
    scores = (
        jnp.einsum("rd,cd->rc", tokens_x, tokens_x, preferred_element_type=jnp.float32) * inv_root
    )
    row_group = jnp.repeat(group, block_rows)
    position = jnp.arange(row_count)
    allowed = (row_group[:, None] == row_group[None, :]) & (position[:, None] != position[None, :])
    scores = jnp.where(allowed, scores, NEG_FILL)
    row_max = jnp.max(scores, axis=1, keepdims=True)
    raised = jnp.exp(scores - row_max)
    weights = raised / jnp.sum(raised, axis=1, keepdims=True)
    attended = jnp.einsum(
        "rc,cd->rd", weights.astype(jnp.bfloat16), tokens_v, preferred_element_type=jnp.float32
    )
    return (weights, attended)


def unit_backward(tokens_x, tokens_v, grad_rows, weights, attended):
    inv_root = tokens_x.shape[1] ** (-0.5)
    grad_weights = jnp.einsum("rd,cd->rc", grad_rows, tokens_v, preferred_element_type=jnp.float32)
    row_delta = jnp.sum(grad_rows.astype(jnp.float32) * attended, axis=1, keepdims=True)
    grad_scores = weights * (grad_weights - row_delta)
    symmetric = (grad_scores + grad_scores.T).astype(jnp.bfloat16)
    grad_x = (
        jnp.einsum("rc,cd->rd", symmetric, tokens_x, preferred_element_type=jnp.float32) * inv_root
    ).astype(jnp.bfloat16)
    grad_v = jnp.einsum(
        "rc,rd->cd", weights.astype(jnp.bfloat16), grad_rows, preferred_element_type=jnp.float32
    ).astype(jnp.bfloat16)
    return (grad_x, grad_v)


def forward_unit(operands):
    tokens_x, tokens_v, group = operands
    return unit_forward(tokens_x, tokens_v, group)


def backward_unit(operands):
    tokens_x, tokens_v, grad_rows, weights, attended = operands
    return unit_backward(tokens_x, tokens_v, grad_rows, weights, attended)


def to_slots(local, packing, seq_count):
    blocks_here = packing.shape[1]
    heads_here = packing.shape[2]
    head_width = local.shape[1] // heads_here
    shaped = local.reshape(blocks_here, BLOCK, heads_here, head_width)
    packed = jnp.einsum(
        "ptk,trkd->prd", packing, shaped, preferred_element_type=jnp.float32
    ).astype(jnp.bfloat16)
    return packed.reshape(seq_count, -1, head_width)


def from_slots(arrived, packing):
    head_width = arrived.shape[-1]
    flat = arrived.reshape(packing.shape[0], BLOCK, head_width)
    placed = jnp.einsum("ptk,prd->trkd", packing, flat, preferred_element_type=jnp.float32).astype(
        jnp.bfloat16
    )
    return placed.reshape(packing.shape[1] * BLOCK, packing.shape[2] * head_width)


def to_units(arrived, picking, unit_count):
    head_width = arrived.shape[-1]
    flat = arrived.reshape(picking.shape[1], BLOCK, head_width)
    gathered = jnp.einsum("up,prd->urd", picking, flat, preferred_element_type=jnp.float32).astype(
        jnp.bfloat16
    )
    return gathered.reshape(unit_count, -1, head_width)


def from_units(results, picking, seq_count):
    head_width = results.shape[-1]
    flat = results.reshape(picking.shape[0], BLOCK, head_width)
    placed = jnp.einsum("up,urd->prd", picking, flat, preferred_element_type=jnp.float32).astype(
        jnp.bfloat16
    )
    return placed.reshape(seq_count, -1, head_width)


def model_output(attended, out_weight):
    partial_term = jnp.dot(attended, out_weight, preferred_element_type=jnp.float32)
    return lax.psum_scatter(
        partial_term.astype(jnp.bfloat16), "head", scatter_dimension=1, tiled=True
    )


def cotangent_heads(out_cotangent, out_weight):
    summed = jnp.einsum(
        "tn,kn->tk",
        lax.all_gather(out_cotangent, "head", axis=1, tiled=True),
        out_weight,
        preferred_element_type=jnp.float32,
    )
    return summed.astype(jnp.bfloat16)


def per_device(qk, values, out_weight, out_cotangent, cluster_ids):
    seq_count = lax.axis_size("seq")
    my_seq = lax.axis_index("seq")
    block_count = cluster_ids.shape[0]
    heads_here = cluster_ids.shape[1]
    blocks_here = qk.shape[0] // BLOCK
    item_count = blocks_here * heads_here
    per_peer = max(2, (item_count + seq_count - 1) // seq_count)
    slot_total = seq_count * per_peer
    owners = cluster_ids // CL_OWN
    item_owner = owners.reshape(seq_count, item_count)
    item_order = jnp.arange(item_count)
    before = item_order[None, :] < item_order[:, None]
    same_owner = item_owner[:, :, None] == item_owner[:, None, :]
    rank_sent = jnp.sum((same_owner & before[None, :, :]).astype(jnp.int32), axis=2)
    slot_index = item_owner * per_peer + rank_sent
    my_slots = lax.dynamic_index_in_dim(slot_index, my_seq, 0, keepdims=False)
    slot_range = jnp.arange(slot_total, dtype=jnp.int32)
    packing = (
        (slot_range[:, None] == my_slots[None, :])
        .astype(jnp.bfloat16)
        .reshape(slot_total, blocks_here, heads_here)
    )
    source_seq = jnp.arange(seq_count, dtype=jnp.int32)[:, None]
    arrival_slot = source_seq * per_peer + rank_sent
    received = (owners == my_seq).T.astype(jnp.int32)
    source_slot = arrival_slot.reshape(block_count, heads_here).T
    position = jnp.cumsum(received, axis=1) - received
    places = jnp.arange(blocks_here, dtype=jnp.int32)
    chosen = (received[:, None, :] == 1) & (position[:, None, :] == places[None, :, None])
    unit_slot = jnp.sum(jnp.where(chosen, source_slot[:, None, :], 0), axis=2)
    unit_group = jnp.sum(jnp.where(chosen, cluster_ids.T[:, None, :], 0), axis=2)
    picking = (unit_slot.reshape(-1)[:, None] == slot_range[None, :]).astype(jnp.bfloat16)
    send_x = to_slots(qk, packing, seq_count)
    send_v = to_slots(values, packing, seq_count)
    arrived_x, arrived_v = (
        lax.all_to_all(send_x, "seq", split_axis=0, concat_axis=0, tiled=True),
        lax.all_to_all(send_v, "seq", split_axis=0, concat_axis=0, tiled=True),
    )
    unit_x = to_units(arrived_x, picking, heads_here)
    unit_v = to_units(arrived_v, picking, heads_here)
    weights, unit_att = lax.map(forward_unit, (unit_x, unit_v, unit_group))
    home_att = lax.all_to_all(
        from_units(unit_att.astype(jnp.bfloat16), picking, seq_count),
        "seq",
        split_axis=0,
        concat_axis=0,
        tiled=True,
    )
    attended = from_slots(home_att, packing)
    output = model_output(attended, out_weight)
    grad_attended = cotangent_heads(out_cotangent, out_weight)
    arrived_g = lax.all_to_all(
        to_slots(grad_attended, packing, seq_count), "seq", split_axis=0, concat_axis=0, tiled=True
    )
    unit_g = to_units(arrived_g, picking, heads_here)
    unit_gx, unit_gv = lax.map(backward_unit, (unit_x, unit_v, unit_g, weights, unit_att))
    home_gx, home_gv = (
        lax.all_to_all(
            from_units(unit_gx, picking, seq_count), "seq", split_axis=0, concat_axis=0, tiled=True
        ),
        lax.all_to_all(
            from_units(unit_gv, picking, seq_count), "seq", split_axis=0, concat_axis=0, tiled=True
        ),
    )
    grad_qk = from_slots(home_gx, packing)
    grad_values = from_slots(home_gv, packing)
    return (output, grad_qk, grad_values)


def solution(mesh):
    return jax.shard_map(
        per_device,
        mesh=mesh,
        in_specs=(
            P("seq", "head"),
            P("seq", "head"),
            P("head", None),
            P("seq", "head"),
            P(None, "head"),
        ),
        out_specs=(P("seq", "head"), P("seq", "head"), P("seq", "head")),
        check_vma=False,
    )
```

profile of v0, /device:TPU:16, one launch (start us, length us, event | category | flops | bytes accessed | tf_op | source)
XLA Modules:
  0.0 683.7 jit_solution(4577155340845065639)
XLA Ops:
  11.8 4.6 copy.60
  16.4 12.2 %all-to-all-start = ((bf16[64,256,128]{2,1,0:T(8,128)(2,1)}), bf16[64,256,128]{2,1,0:T(8,128)(2,1)}, u32[]{:S(2)}, u32[]{:S(2)}) async-start(bf16[64,256,128]{2,1,0:T(8,128)(2,1)} %bitcast.193), calls=%async_computation | async-start | bytes 8388608 | tf_op jit(solution)/shard_map/all_to_all | solution.py:147
  31.4 4.7 copy.64
  36.0 88.8 %all-to-all-done = bf16[64,256,128]{2,1,0:T(8,128)(2,1)} async-done(((bf16[64,256,128]{2,1,0:T(8,128)(2,1)}), bf16[64,256,128]{2,1,0:T(8,128)(2,1)}, u32[]{:S(2)}, u32[]{:S(2)}) %all-to-all-start) | async-done | bytes 4194336 | tf_op jit(solution)/shard_map/all_to_all | solution.py:147
  124.8 5.8 all-to-all-start.1
  134.1 50.2 %all-gather.2.cloned.1.call-done = bf16[1024,2048]{1,0:T(8,128)(2,1)} async-done(((bf16[1024,512]{1,0:T(8,128)(2,1)}), bf16[1024,2048]{1,0:T(8,128)(2,1)}) %all-gather.2.cloned.1.call-update) | async-done | bytes 4194320 | tf_op jit(solution)/shard_map/all_gather | solution.py:104
  184.3 5.5 convolution_convert_fusion.4
  192.6 4.6 copy.73
  197.2 4.8 fusion.70
  202.4 24.5 %all-to-all-done.1 = bf16[64,256,128]{2,1,0:T(8,128)(2,1)} async-done(((bf16[64,256,128]{2,1,0:T(8,128)(2,1)}), bf16[64,256,128]{2,1,0:T(8,128)(2,1)}, u32[]{:S(2)}, u32[]{:S(2)}) %all-to-all-start.1) | async-done | bytes 4194336 | tf_op jit(solution)/shard_map/all_to_all | solution.py:148
  226.9 6.1 all-to-all-start.3
  233.0 4.8 fusion.73
  239.2 27.8 %while.24 = (s32[]{:T(128)}, f32[4,1024,1024]{1,2,0:T(8,128)}, f32[4,1024,128]{2,1,0:T(8,128)}, s32[4,8]{1,0:T(4,128)S(1)}, bf16[4,1024,128]{2,1,0:T(8,128)(2,1)S(1)}, /*index=5*/bf16[4,1024,128]{2,1,0:T(8,128)(2,1)}, s32[]{:T(128)}) while((s32[]{:T(128)}, f32[4,1024,1024]{1,2,0:T(8,128)}, f32[4,1024,128]{2,1,0:T(8,128)}, ...), condition=%wide.region_8.9_spmd, body=%wide.region_5.8_spmd.sunk | while | flops 550500352 | bytes 22062772 | solution.py:152
  241.0 2.5 bitcast_dynamic-update-slice_fusion.2
  243.5 2.6 fusion.160
  247.9 2.5 bitcast_dynamic-update-slice_fusion.2
  250.5 2.6 fusion.160
  254.9 2.5 bitcast_dynamic-update-slice_fusion.2
  257.4 2.6 fusion.160
  261.8 2.5 bitcast_dynamic-update-slice_fusion.2
  264.4 2.6 fusion.160
  266.9 2.1 convert_element_type.93
  270.4 4.7 copy.68
  275.1 54.1 %all-to-all-done.3 = bf16[64,256,128]{2,1,0:T(8,128)(2,1)} async-done(((bf16[64,256,128]{2,1,0:T(8,128)(2,1)}), bf16[64,256,128]{2,1,0:T(8,128)(2,1)}, u32[]{:S(2)}, u32[]{:S(2)}) %all-to-all-start.3) | async-done | bytes 4194336 | tf_op jit(solution)/shard_map/all_to_all | solution.py:163
  329.2 5.8 all-to-all-start.2
  335.0 4.8 fusion.76
  340.3 112.8 %while.25 = (s32[]{:T(128)}, bf16[4,1024,128]{2,1,0:T(8,128)(2,1)}, bf16[4,1024,128]{2,1,0:T(8,128)(2,1)}, f32[4,1024,1024]{1,2,0:T(8,128)}, bf16[4,1024,128]{2,...) while((s32[]{:T(128)}, bf16[4,1024,128]{2,1,0:T(8,128)(2,1)}, ...), condition=%wide.region_12.13_spmd, body=%wide.region_10.12_spmd.sunk | while | flops 811334656 | bytes 65285248 | solution.py:167
  341.5 4.7 constant_dynamic-slice_fusion.3
  346.3 5.3 copy.159
  351.6 4.9 bitcast_multiply_fusion.3
  356.5 5.4 copy.160
  361.9 5.1 fusion.168
  367.0 1.5 fusion.169
  369.7 4.7 constant_dynamic-slice_fusion.3
  374.5 5.3 copy.159
  379.8 4.9 bitcast_multiply_fusion.3
  384.7 5.4 copy.160
  390.1 5.1 fusion.168
  395.2 1.5 fusion.169
  397.9 4.7 constant_dynamic-slice_fusion.3
  402.7 5.3 copy.159
  408.0 4.9 bitcast_multiply_fusion.3
  412.9 5.4 copy.160
  418.3 5.1 fusion.168
  423.4 1.5 fusion.169
  426.1 4.7 constant_dynamic-slice_fusion.3
  430.9 5.3 copy.159
  436.2 4.9 bitcast_multiply_fusion.3
  441.1 5.4 copy.160
  446.5 5.1 fusion.168
  453.1 2.6 convolution_convert_fusion.2
  455.7 4.7 copy.78
  460.4 10.9 %all-to-all-start.4 = ((bf16[64,256,128]{2,1,0:T(8,128)(2,1)}), bf16[64,256,128]{2,1,0:T(8,128)(2,1)}, u32[]{:S(2)}, u32[]{:S(2)}) async-start(bf16[64,256,128]{2,1,0:T(8,128)(2,1)} %bitcast.192), calls=%async_computation.5 | async-start | bytes 8388608 | tf_op jit(solution)/shard_map/all_to_all | solution.py:169
  471.2 2.6 convolution_convert_fusion.1
  473.8 4.7 copy.82
  478.5 88.9 %all-to-all-done.4 = bf16[64,256,128]{2,1,0:T(8,128)(2,1)} async-done(((bf16[64,256,128]{2,1,0:T(8,128)(2,1)}), bf16[64,256,128]{2,1,0:T(8,128)(2,1)}, u32[]{:S(2)}, u32[]{:S(2)}) %all-to-all-start.4) | async-done | bytes 4194336 | tf_op jit(solution)/shard_map/all_to_all | solution.py:169
  567.5 5.8 all-to-all-start.5
  573.3 4.8 fusion.94
  578.1 2.0 copy.71
  580.1 5.6 convolution_convert_fusion
  585.7 4.8 fusion.91
  591.0 78.5 %all-to-all-done.5 = bf16[64,256,128]{2,1,0:T(8,128)(2,1)} async-done(((bf16[64,256,128]{2,1,0:T(8,128)(2,1)}), bf16[64,256,128]{2,1,0:T(8,128)(2,1)}, u32[]{:S(2)}, u32[]{:S(2)}) %all-to-all-start.5) | async-done | bytes 4194336 | tf_op jit(solution)/shard_map/all_to_all | solution.py:172
  669.5 4.8 fusion.88
  674.7 1.7 copy_bitcast_fusion
  (85 shorter events, 31.7 us)
Async XLA Ops:
  7.2 177.1 %copy-start = (bf16[512,2048]{1,0:T(8,128)(2,1)S(1)}, bf16[512,2048]{1,0:T(8,128)(2,1)}, u32[]{:S(2)}) copy-start(bf16[512,2048]{1,0:T(8,128)(2,1)} %param.11) | copy-start | bytes 6291460
  9.0 182.1 %copy-start.3 = (s32[8,4]{0,1:T(4,128)}, s32[8,4]{0,1:T(4,128)S(1)}, u32[]{:S(2)}) copy-start(s32[8,4]{0,1:T(4,128)S(1)} %copy.58) | copy-start | bytes 388
  16.4 108.4 %all-to-all-start = ((bf16[64,256,128]{2,1,0:T(8,128)(2,1)}), bf16[64,256,128]{2,1,0:T(8,128)(2,1)}, u32[]{:S(2)}, u32[]{:S(2)}) async-start(bf16[64,256,128]{2,1,0:T(8,128)(2,1)} %bitcast.193), calls=%async_computation | async-start | bytes 8388608 | tf_op jit(solution)/shard_map/all_to_all | solution.py:147
  124.8 8.9 %copy-start.5 = (s32[512,4]{0,1:T(4,128)S(1)}, s32[512,4]{0,1:T(4,128)}, u32[]{:S(2)}) copy-start(s32[512,4]{0,1:T(4,128)} %param.13) | copy-start | bytes 24580
  124.8 102.0 %all-to-all-start.1 = ((bf16[64,256,128]{2,1,0:T(8,128)(2,1)}), bf16[64,256,128]{2,1,0:T(8,128)(2,1)}, u32[]{:S(2)}, u32[]{:S(2)}) async-start(bf16[64,256,128]{2,1,0:T(8,128)(2,1)} %bitcast.190), calls=%async_computation.1 | async-start | bytes 8388608 | tf_op jit(solution)/shard_map/all_to_all | solution.py:148
  130.6 53.7 %all-gather.2.cloned.1.call-start = ((), (), s32[]{:S(2)}) async-start(), calls=%async_computation.8 | async-start | bytes 5242880 | tf_op jit(solution)/shard_map/all_gather | solution.py:104
  226.9 102.3 %all-to-all-start.3 = ((bf16[64,256,128]{2,1,0:T(8,128)(2,1)}), bf16[64,256,128]{2,1,0:T(8,128)(2,1)}, u32[]{:S(2)}, u32[]{:S(2)}) async-start(bf16[64,256,128]{2,1,0:T(8,128)(2,1)} %bitcast.188), calls=%async_computation.4 | async-start | bytes 8388608 | tf_op jit(solution)/shard_map/all_to_all | solution.py:163
  266.9 3.5 copy-start.2
  329.2 131.2 %all-to-all-start.2 = ((bf16[64,256,128]{2,1,0:T(8,128)(2,1)}), bf16[64,256,128]{2,1,0:T(8,128)(2,1)}, u32[]{:S(2)}, u32[]{:S(2)}) async-start(bf16[64,256,128]{2,1,0:T(8,128)(2,1)} %bitcast.189), calls=%async_computation.2 | async-start | bytes 8388608 | tf_op jit(solution)/shard_map/all_to_all | solution.py:153
  361.9 5.1 copy-start.1
  390.1 5.1 copy-start.1
  418.3 5.1 copy-start.1
  446.5 5.1 copy-start.1
  460.4 107.1 %all-to-all-start.4 = ((bf16[64,256,128]{2,1,0:T(8,128)(2,1)}), bf16[64,256,128]{2,1,0:T(8,128)(2,1)}, u32[]{:S(2)}, u32[]{:S(2)}) async-start(bf16[64,256,128]{2,1,0:T(8,128)(2,1)} %bitcast.192), calls=%async_computation.5 | async-start | bytes 8388608 | tf_op jit(solution)/shard_map/all_to_all | solution.py:169
  567.4 5.9 copy-start.4
  567.5 102.0 %all-to-all-start.5 = ((bf16[64,256,128]{2,1,0:T(8,128)(2,1)}), bf16[64,256,128]{2,1,0:T(8,128)(2,1)}, u32[]{:S(2)}, u32[]{:S(2)}) async-start(bf16[64,256,128]{2,1,0:T(8,128)(2,1)} %bitcast.191), calls=%async_computation.6 | async-start | bytes 8388608 | tf_op jit(solution)/shard_map/all_to_all | solution.py:172
  573.3 103.2 %reduce-scatter.2.cloned.1.call-start = ((), (), s32[]{:S(2)}) async-start(), calls=%async_computation.7 | async-start | bytes 5242880 | tf_op jit(solution)/shard_map/reduce_scatter | solution.py:96
Sparse Core Ops, SparseCore 0:
  133.3 50.9 all-gather.1
  585.8 48.8 reduce-scatter.1
where the time goes:
time: 694 us; the launch traced here: 684 us
  waiting for transfers between devices  386 us (56%)
  matrix products  111 us (16%)
  local copies, waits for them, and re-layouts  102 us (15%)
  starting transfers between devices  46.9 us (7%)
  other arithmetic  22.8 us (3%)
  between operations  14.8 us (2%)
    all_to_all x1, waiting for transfers between devices, per_device(): lax.all_to_all(from_units(unit_gx, picking, seq_count), 'seq', split_axis...  88.9 us
    all_to_all x1, waiting for transfers between devices, per_device(): lax.all_to_all(send_x, 'seq', split_axis=0, concat_axis=0, tiled=True)  88.8 us
    all_to_all x1, waiting for transfers between devices, per_device(): lax.all_to_all(from_units(unit_gv, picking, seq_count), 'seq', split_axis...  78.5 us
    all_to_all x1, waiting for transfers between devices, per_device(): lax.all_to_all(to_slots(grad_attended, packing, seq_count), 'seq', split_...  54.1 us
    all_gather x1, waiting for transfers between devices, cotangent_heads(): lax.all_gather(out_cotangent, 'head', axis=1, tiled=True)  50.2 us
    dynamic_slice x8, local copies, waits for them, and re-layouts, per_device(): lax.map(backward_unit, (unit_x, unit_v, unit_g, weights, unit_att))  40.2 us
    all_to_all x1, waiting for transfers between devices, per_device(): lax.all_to_all(send_v, 'seq', split_axis=0, concat_axis=0, tiled=True)  24.5 us
    mul x4, local copies, waits for them, and re-layouts, unit_backward(): grad_scores = weights * (grad_weights - row_delta)  21.5 us
  transfers between devices with their start and end apart: 8, of which 6 were waited for; matrix products, arithmetic and copies ran while one was open for 33% of the time, Pallas kernels for 0%

commit v1 on v0

--- a/solution.py
+++ b/solution.py
@@ -1,3 +1,4 @@
+import functools
 import jax
 import jax.numpy as jnp
 from jax import lax
@@ -6,6 +7,24 @@
 BLOCK = 128
 CL_OWN = 2
 NEG_FILL = -1e30
+
+
+def remake_patches(xx, k_dim):
+    nodes = jax.lax.axis_size("head")
+    xs_all = tuple(((src_i, (src_i + 1) % nodes) for src_i in range(nodes)))
+    views = tuple(((src_i, (src_i - 1) % nodes) for src_i in range(nodes)))
+    after, block_now = ([xx], [xx])
+    for _ in range(nodes // 2):
+        after.append(jax.lax.ppermute(after[-1], "head", xs_all))
+    for _ in [*range((nodes - 1) // 2)]:
+        block_now.append(jax.lax.ppermute(block_now[-1], "head", views))
+    far_arr = jnp.concatenate([*after[::-1], *block_now[1:]], k_dim)
+    w1 = jax.lax.axis_index("head")
+    newest = jnp.roll(far_arr, (w1 - nodes // 2) * xx.shape[k_dim], k_dim)
+    return newest
+
+
+move_racks = functools.partial(remake_patches, k_dim=1)
 
 
 def unit_forward(tokens_x, tokens_v, group):
@@ -100,10 +119,7 @@
 
 def cotangent_heads(out_cotangent, out_weight):
     summed = jnp.einsum(
-        "tn,kn->tk",
-        lax.all_gather(out_cotangent, "head", axis=1, tiled=True),
-        out_weight,
-        preferred_element_type=jnp.float32,
+        "tn,kn->tk", move_racks(out_cotangent), out_weight, preferred_element_type=jnp.float32
     )
     return summed.astype(jnp.bfloat16)
 

time: 694 us -> 694 us (level)
  waiting for transfers between devices: 386 us -> 374 us
  local copies, waits for them, and re-layouts: 102 us -> 112 us
    all_gather x1 -> x0, waiting for transfers between devices: 50.2 us -> none  [cotangent_heads(): lax.all_gather(out_cotangent, 'head', axis=1, tiled=True)]
    ppermute x0 -> x3, waiting for transfers between devices: none -> 41.8 us  [the longest x2 41.7 us: remake_patches(): after.append(jax.lax.ppermute(after[-1], 'head', xs_all))]
    unnamed x13 -> x22, local copies, waits for them, and re-layouts: 2.59 us -> 9.78 us
  transfers between devices with their start and end apart: 8 -> 10, of which waited for: 6 -> 7; matrix products, arithmetic and copies ran while one was open for 33% -> 34% of each run, Pallas kernels for 0% -> 0%
where the time goes in v1:
time: 694 us; the launch traced here: 684 us
  waiting for transfers between devices  374 us (54%)
  local copies, waits for them, and re-layouts  112 us (16%)
  matrix products  109 us (16%)
  starting transfers between devices  50.2 us (7%)
  other arithmetic  23.5 us (3%)
  between operations  14.8 us (2%)
    all_to_all x1, waiting for transfers between devices, per_device(): lax.all_to_all(from_units(unit_gx, picking, seq_count), 'seq', split_axis...  88.9 us
    all_to_all x1, waiting for transfers between devices, per_device(): lax.all_to_all(send_x, 'seq', split_axis=0, concat_axis=0, tiled=True)  88.8 us
    all_to_all x1, waiting for transfers between devices, per_device(): lax.all_to_all(from_units(unit_gv, picking, seq_count), 'seq', split_axis...  78.5 us
    all_to_all x1, waiting for transfers between devices, per_device(): lax.all_to_all(to_slots(grad_attended, packing, seq_count), 'seq', split_...  54.1 us
    ppermute x2, waiting for transfers between devices, remake_patches(): after.append(jax.lax.ppermute(after[-1], 'head', xs_all))  41.7 us
    dynamic_slice x8, local copies, waits for them, and re-layouts, per_device(): lax.map(backward_unit, (unit_x, unit_v, unit_g, weights, unit_att))  40.2 us
    all_to_all x1, waiting for transfers between devices, per_device(): lax.all_to_all(send_v, 'seq', split_axis=0, concat_axis=0, tiled=True)  22 us
    mul x4, local copies, waits for them, and re-layouts, unit_backward(): grad_scores = weights * (grad_weights - row_delta)  21.5 us
  transfers between devices with their start and end apart: 10, of which 7 were waited for; matrix products, arithmetic and copies ran while one was open for 34% of the time, Pallas kernels for 0%

profile of v1, /device:TPU:16, one launch (start us, length us, event | category | flops | bytes accessed | tf_op | source)
XLA Modules:
  0.0 683.7 jit_solution(15613215929372805065)
XLA Ops:
  11.8 4.6 copy.60
  16.4 12.2 %all-to-all-start = ((bf16[64,256,128]{2,1,0:T(8,128)(2,1)}), bf16[64,256,128]{2,1,0:T(8,128)(2,1)}, u32[]{:S(2)}, u32[]{:S(2)}) async-start(bf16[64,256,128]{2,1,0:T(8,128)(2,1)} %bitcast.192), calls=%async_computation | async-start | bytes 8388608 | tf_op jit(solution)/shard_map/all_to_all | solution.py:163
  31.4 4.7 copy.64
  36.0 88.8 %all-to-all-done = bf16[64,256,128]{2,1,0:T(8,128)(2,1)} async-done(((bf16[64,256,128]{2,1,0:T(8,128)(2,1)}), bf16[64,256,128]{2,1,0:T(8,128)(2,1)}, u32[]{:S(2)}, u32[]{:S(2)}) %all-to-all-start) | async-done | bytes 4194336 | tf_op jit(solution)/shard_map/all_to_all | solution.py:163
  124.8 5.8 all-to-all-start.1
  130.7 1.5 collective-permute-start
  132.2 23.8 %collective-permute-done = bf16[1024,512]{1,0:T(8,128)(2,1)} collective-permute-done((bf16[1024,512]{1,0:T(8,128)(2,1)S(1)}, bf16[1024,512]{1,0:T(8,128)(2,1)}, u32[]{:S(2)}, u32[]{:S(2)}) %collective-permute-start) | collective-permute-done | bytes 1048608 | tf_op jit(solution)/shard_map/ppermute | solution.py:18
  162.3 18.0 %collective-permute-done.1 = bf16[1024,512]{1,0:T(8,128)(2,1)} collective-permute-done((bf16[1024,512]{1,0:T(8,128)(2,1)}, bf16[1024,512]{1,0:T(8,128)(2,1)}, u32[]{:S(2)}, u32[]{:S(2)}) %collective-permute-start.1) | collective-permute-done | bytes 1048608 | tf_op jit(solution)/shard_map/ppermute | solution.py:18
  189.0 3.3 fusion.90
  195.1 4.6 copy.73
  199.7 4.8 fusion.72
  204.9 22.0 %all-to-all-done.1 = bf16[64,256,128]{2,1,0:T(8,128)(2,1)} async-done(((bf16[64,256,128]{2,1,0:T(8,128)(2,1)}), bf16[64,256,128]{2,1,0:T(8,128)(2,1)}, u32[]{:S(2)}, u32[]{:S(2)}) %all-to-all-start.1) | async-done | bytes 4194336 | tf_op jit(solution)/shard_map/all_to_all | solution.py:164
  226.9 6.1 all-to-all-start.3
  233.0 4.8 fusion.75
  239.2 27.8 %while.24 = (s32[]{:T(128)}, f32[4,1024,1024]{1,2,0:T(8,128)}, f32[4,1024,128]{2,1,0:T(8,128)}, s32[4,8]{1,0:T(4,128)S(1)}, bf16[4,1024,128]{2,1,0:T(8,128)(2,1)S(1)}, /*index=5*/bf16[4,1024,128]{2,1,0:T(8,128)(2,1)}, s32[]{:T(128)}) while((s32[]{:T(128)}, f32[4,1024,1024]{1,2,0:T(8,128)}, f32[4,1024,128]{2,1,0:T(8,128)}, ...), condition=%wide.region_8.9_spmd, body=%wide.region_5.8_spmd.sunk | while | flops 550500352 | bytes 22062772 | solution.py:168
  241.0 2.5 bitcast_dynamic-update-slice_fusion.2
  243.5 2.6 fusion.165
  247.9 2.5 bitcast_dynamic-update-slice_fusion.2
  250.5 2.6 fusion.165
  254.9 2.5 bitcast_dynamic-update-slice_fusion.2
  257.4 2.6 fusion.165
  261.9 2.5 bitcast_dynamic-update-slice_fusion.2
  264.4 2.6 fusion.165
  266.9 2.1 convert_element_type.93
  270.4 4.7 copy.68
  275.1 54.1 %all-to-all-done.3 = bf16[64,256,128]{2,1,0:T(8,128)(2,1)} async-done(((bf16[64,256,128]{2,1,0:T(8,128)(2,1)}), bf16[64,256,128]{2,1,0:T(8,128)(2,1)}, u32[]{:S(2)}, u32[]{:S(2)}) %all-to-all-start.3) | async-done | bytes 4194336 | tf_op jit(solution)/shard_map/all_to_all | solution.py:179
  329.2 5.8 all-to-all-start.2
  335.0 4.8 fusion.78
  340.3 112.8 %while.25 = (s32[]{:T(128)}, bf16[4,1024,128]{2,1,0:T(8,128)(2,1)}, bf16[4,1024,128]{2,1,0:T(8,128)(2,1)}, f32[4,1024,1024]{1,2,0:T(8,128)}, bf16[4,1024,128]{2,...) while((s32[]{:T(128)}, bf16[4,1024,128]{2,1,0:T(8,128)(2,1)}, ...), condition=%wide.region_12.13_spmd, body=%wide.region_10.12_spmd.sunk | while | flops 811334656 | bytes 65285248 | solution.py:183
  341.5 4.7 constant_dynamic-slice_fusion.3
  346.3 5.3 copy.159
  351.6 4.9 bitcast_multiply_fusion.3
  356.5 5.4 copy.160
  361.9 5.1 fusion.173
  369.7 4.7 constant_dynamic-slice_fusion.3
  374.5 5.3 copy.159
  379.8 4.9 bitcast_multiply_fusion.3
  384.7 5.4 copy.160
  390.1 5.1 fusion.173
  397.9 4.7 constant_dynamic-slice_fusion.3
  402.7 5.3 copy.159
  408.0 4.9 bitcast_multiply_fusion.3
  412.9 5.4 copy.160
  418.3 5.1 fusion.173
  423.4 1.5 fusion.174
  426.1 4.7 constant_dynamic-slice_fusion.3
  430.9 5.3 copy.159
  436.2 4.9 bitcast_multiply_fusion.3
  441.1 5.4 copy.160
  446.5 5.1 fusion.173
  453.1 2.6 convolution_convert_fusion.2
  455.7 4.7 copy.78
  460.3 10.9 %all-to-all-start.4 = ((bf16[64,256,128]{2,1,0:T(8,128)(2,1)}), bf16[64,256,128]{2,1,0:T(8,128)(2,1)}, u32[]{:S(2)}, u32[]{:S(2)}) async-start(bf16[64,256,128]{2,1,0:T(8,128)(2,1)} %bitcast.191), calls=%async_computation.5 | async-start | bytes 8388608 | tf_op jit(solution)/shard_map/all_to_all | solution.py:185
  471.3 2.6 convolution_convert_fusion.1
  473.9 4.7 copy.82
  478.6 88.9 %all-to-all-done.4 = bf16[64,256,128]{2,1,0:T(8,128)(2,1)} async-done(((bf16[64,256,128]{2,1,0:T(8,128)(2,1)}), bf16[64,256,128]{2,1,0:T(8,128)(2,1)}, u32[]{:S(2)}, u32[]{:S(2)}) %all-to-all-start.4) | async-done | bytes 4194336 | tf_op jit(solution)/shard_map/all_to_all | solution.py:185
  567.5 5.8 all-to-all-start.5
  573.4 4.8 fusion.99
  578.2 2.0 copy.71
  580.2 5.6 convolution_convert_fusion
  585.8 4.8 fusion.96
  591.0 78.5 %all-to-all-done.5 = bf16[64,256,128]{2,1,0:T(8,128)(2,1)} async-done(((bf16[64,256,128]{2,1,0:T(8,128)(2,1)}), bf16[64,256,128]{2,1,0:T(8,128)(2,1)}, u32[]{:S(2)}, u32[]{:S(2)}) %all-to-all-start.5) | async-done | bytes 4194336 | tf_op jit(solution)/shard_map/all_to_all | solution.py:188
  669.5 4.8 fusion.93
  674.8 1.7 copy_bitcast_fusion
  (98 shorter events, 46.2 us)
Async XLA Ops:
  7.2 181.8 %copy-start = (bf16[512,2048]{1,0:T(8,128)(2,1)S(1)}, bf16[512,2048]{1,0:T(8,128)(2,1)}, u32[]{:S(2)}) copy-start(bf16[512,2048]{1,0:T(8,128)(2,1)} %param.11) | copy-start | bytes 6291460
  9.0 184.6 %copy-start.4 = (s32[8,4]{0,1:T(4,128)}, s32[8,4]{0,1:T(4,128)S(1)}, u32[]{:S(2)}) copy-start(s32[8,4]{0,1:T(4,128)S(1)} %copy.58) | copy-start | bytes 388
  16.4 108.4 %all-to-all-start = ((bf16[64,256,128]{2,1,0:T(8,128)(2,1)}), bf16[64,256,128]{2,1,0:T(8,128)(2,1)}, u32[]{:S(2)}, u32[]{:S(2)}) async-start(bf16[64,256,128]{2,1,0:T(8,128)(2,1)} %bitcast.192), calls=%async_computation | async-start | bytes 8388608 | tf_op jit(solution)/shard_map/all_to_all | solution.py:163
  124.8 5.8 copy-start.3
  124.8 37.2 %copy-start.6 = (s32[512,4]{0,1:T(4,128)S(1)}, s32[512,4]{0,1:T(4,128)}, u32[]{:S(2)}) copy-start(s32[512,4]{0,1:T(4,128)} %param.13) | copy-start | bytes 24580
  124.8 102.0 %all-to-all-start.1 = ((bf16[64,256,128]{2,1,0:T(8,128)(2,1)}), bf16[64,256,128]{2,1,0:T(8,128)(2,1)}, u32[]{:S(2)}, u32[]{:S(2)}) async-start(bf16[64,256,128]{2,1,0:T(8,128)(2,1)} %bitcast.187), calls=%async_computation.1 | async-start | bytes 8388608 | tf_op jit(solution)/shard_map/all_to_all | solution.py:164
  130.7 25.3 %collective-permute-start = (bf16[1024,512]{1,0:T(8,128)(2,1)S(1)}, bf16[1024,512]{1,0:T(8,128)(2,1)}, u32[]{:S(2)}, u32[]{:S(2)}) collective-permute-start(bf16[1024,512]{1,0:T(8,128)(2,1)S(1)} %copy-done.3), channel_id=1, source_target_pairs={{0,1},{1,2},{2,3},{3,0},{4,5},{5,6},{6,7},{7,4},{8,9},{9,10},{10,1... | collective-permute-start | bytes 3145736 | tf_op jit(solution)/shard_map/ppermute | solution.py:18
  155.9 24.4 %collective-permute-start.1 = (bf16[1024,512]{1,0:T(8,128)(2,1)}, bf16[1024,512]{1,0:T(8,128)(2,1)}, u32[]{:S(2)}, u32[]{:S(2)}) collective-permute-start(bf16[1024,512]{1,0:T(8,128)(2,1)} %collective-permute-done), channel_id=1, source_target_pairs={{0,1},{1,2},{2,3},{3,0},{4,5},{5,6},{6,7},{7,4},{8,9},{9,10},{10,1... | collective-permute-start | bytes 3145736 | tf_op jit(solution)/shard_map/ppermute | solution.py:18
  157.2 26.0 %collective-permute-start.2 = (bf16[1024,512]{1,0:T(8,128)(2,1)S(1)}, bf16[1024,512]{1,0:T(8,128)(2,1)}, u32[]{:S(2)}, u32[]{:S(2)}) collective-permute-start(bf16[1024,512]{1,0:T(8,128)(2,1)S(1)} %copy-done.3), channel_id=1, source_target_pairs={{0,3},{1,0},{2,1},{3,2},{4,7},{5,4},{6,5},{7,6},{8,11},{9,8},{10,9... | collective-permute-start | bytes 3145736 | tf_op jit(solution)/shard_map/ppermute | solution.py:20
  226.9 102.3 %all-to-all-start.3 = ((bf16[64,256,128]{2,1,0:T(8,128)(2,1)}), bf16[64,256,128]{2,1,0:T(8,128)(2,1)}, u32[]{:S(2)}, u32[]{:S(2)}) async-start(bf16[64,256,128]{2,1,0:T(8,128)(2,1)} %bitcast.188), calls=%async_computation.4 | async-start | bytes 8388608 | tf_op jit(solution)/shard_map/all_to_all | solution.py:179
  266.9 3.5 copy-start.2
  329.2 131.2 %all-to-all-start.2 = ((bf16[64,256,128]{2,1,0:T(8,128)(2,1)}), bf16[64,256,128]{2,1,0:T(8,128)(2,1)}, u32[]{:S(2)}, u32[]{:S(2)}) async-start(bf16[64,256,128]{2,1,0:T(8,128)(2,1)} %bitcast.189), calls=%async_computation.2 | async-start | bytes 8388608 | tf_op jit(solution)/shard_map/all_to_all | solution.py:169
  361.9 5.1 copy-start.1
  390.1 5.1 copy-start.1
  418.3 5.1 copy-start.1
  446.5 5.1 copy-start.1
  460.3 107.1 %all-to-all-start.4 = ((bf16[64,256,128]{2,1,0:T(8,128)(2,1)}), bf16[64,256,128]{2,1,0:T(8,128)(2,1)}, u32[]{:S(2)}, u32[]{:S(2)}) async-start(bf16[64,256,128]{2,1,0:T(8,128)(2,1)} %bitcast.191), calls=%async_computation.5 | async-start | bytes 8388608 | tf_op jit(solution)/shard_map/all_to_all | solution.py:185
  567.5 5.9 copy-start.5
  567.5 102.0 %all-to-all-start.5 = ((bf16[64,256,128]{2,1,0:T(8,128)(2,1)}), bf16[64,256,128]{2,1,0:T(8,128)(2,1)}, u32[]{:S(2)}, u32[]{:S(2)}) async-start(bf16[64,256,128]{2,1,0:T(8,128)(2,1)} %bitcast.190), calls=%async_computation.6 | async-start | bytes 8388608 | tf_op jit(solution)/shard_map/all_to_all | solution.py:188
  573.3 103.2 %reduce-scatter.2.cloned.1.call-start = ((), (), s32[]{:S(2)}) async-start(), calls=%async_computation.7 | async-start | bytes 5242880 | tf_op jit(solution)/shard_map/reduce_scatter | solution.py:115
Sparse Core Ops, SparseCore 0:
  585.9 48.8 reduce-scatter.1
